TPU v7x, 256 devices: a whole 4x4x8 slice. The times are simulated.
256 devices in a mesh: guide: 2 (over z_lo), seq: 32 (over x, y, core), tp: 4 (over z_hi).
Axes of the slice: x: 4, y: 4, z: 8 (z_hi: 4, z_lo: 2; z = z_hi * 2 + z_lo), core: 2. Of those that a mesh axis runs over, the one named last changes fastest.
Arguments:
- hidden: bfloat16 [2048, 3072], P('seq', 'tp'), may hold values from -6 to 6
- seg_ids: int32 [2048], P('seq'), may hold values from 0 to 3, never falling along the last dimension, each value on 1 to 769 neighbouring positions
- modulation: bfloat16 [2, 4, 3, 3072], P('guide'), may hold values from -4 to 4
- qk_gain: float32 [2, 128], replicated, may hold values from 0.5 to 5
- w_qkv: bfloat16 [3072, 3, 1536], P(None, None, 'tp'), may hold values from -0.109375 to 0.109375
- w_mlp_in: bfloat16 [3072, 6144], P('seq', 'tp'), may hold values from -0.109375 to 0.109375
- w_out: bfloat16 [1536, 3072], P('tp'), may hold values from -0.5 to 0.5
- w_mlp_back: bfloat16 [3072, 6144], P('seq', 'tp'), may hold values from -0.078125 to 0.078125
Outputs:
- guided: bfloat16 [2048, 4, 2, 384], P('seq', 'tp', 'guide')
Inputs may be any that keep to these rules, and one draw needn't show every extreme that they name: `seg_ids`: 4 requests lie end to end in order; each holds 1 to 769 rows and one holds exactly 769.
All inputs are finite; a program needn't handle non-finite values.
Results may differ from a plain program's by a relative error of at most 0.014.
The roundings to bfloat16 on the way count: a program that leaves them out, or rounds other values in their place, can miss the bound.
Values may be sent and summed in bfloat16 or wider, within the bound.
A program may use at most 128 MiB of HBM per device.

v0:
```python
import jax
import jax.numpy as jnp
from jax import lax
from jax.sharding import PartitionSpec as P

D = 3072
HEAD = 128
guidance = 3.5


def from_partner(block, axis, apart):
    count = lax.axis_size(axis)
    route = []
    for low in range(count):
        high = low | 1 << apart
        if high != low and high < count:
            route += [(low, high), (high, low)]
    return lax.ppermute(block, axis, route)


def head_norm(values, gain):
    return values * lax.rsqrt(jnp.mean(values * values, axis=-1, keepdims=True) + 1e-06) * gain


def on_device(hidden, seg_ids, modulation, qk_gain, w_qkv, w_mlp_in, w_out, w_mlp_back):
    rows = hidden.shape[0]
    local_width = hidden.shape[1]
    group = w_out.shape[0]
    heads_here = group // HEAD
    requests = modulation.shape[1]
    tp_index = lax.axis_index("tp")
    full = lax.all_gather(hidden, "tp", axis=1, tiled=True)
    xf = full.astype(jnp.float32)
    centred = xf - jnp.mean(xf, axis=-1, keepdims=True)
    normed = centred * lax.rsqrt(jnp.mean(centred * centred, axis=-1, keepdims=True) + 1e-06)
    one_hot = (seg_ids[:, None] == lax.iota(jnp.int32, requests)[None, :]).astype(jnp.bfloat16)
    table = modulation[0, :, 0:2, :].reshape(requests, 2 * D)
    looked = jnp.dot(one_hot, table, preferred_element_type=jnp.float32)
    xmod = (normed * (1.0 + looked[:, D:]) + looked[:, :D]).astype(jnp.bfloat16)
    gate_table = lax.dynamic_slice_in_dim(
        modulation[0, :, 2, :], tp_index * local_width, local_width, 1
    )
    gate = jnp.dot(one_hot, gate_table, preferred_element_type=jnp.float32)
    mlp_pre = jnp.dot(
        xmod,
        lax.all_gather(w_mlp_in, "seq", axis=0, tiled=True),
        preferred_element_type=jnp.float32,
    )
    mlp_act = jax.nn.gelu(mlp_pre, approximate=True).astype(jnp.bfloat16)
    proj = jnp.einsum("td,dck->tck", xmod, w_qkv, preferred_element_type=jnp.float32)
    query = head_norm(proj[:, 0].reshape(rows, heads_here, HEAD), qk_gain[0]).astype(jnp.bfloat16)
    key_rows = head_norm(proj[:, 1].reshape(rows, heads_here, HEAD), qk_gain[1]).astype(
        jnp.bfloat16
    )
    value_rows = proj[:, 2].astype(jnp.bfloat16)
    packed = jnp.concatenate([key_rows.reshape(rows, group), value_rows], axis=1)
    seg_plus = seg_ids + 1
    keys_all = lax.all_gather(packed, "seq", axis=0, tiled=True)
    seg_all = lax.all_gather(seg_plus, "seq", axis=0, tiled=True)
    count = keys_all.shape[0]
    keys = keys_all[:, :group].reshape(count, heads_here, HEAD)
    values = keys_all[:, group:].reshape(count, heads_here, HEAD)
    score = jnp.einsum("qhe,khe->hqk", query, keys, preferred_element_type=jnp.float32) * HEAD ** (
        -0.5
    )
    score = jnp.where((seg_plus[:, None] == seg_all[None, :])[None], score, -1e30)
    peak = jnp.max(score, axis=-1, keepdims=True)
    weight = jnp.exp(score - peak)
    total = jnp.sum(weight, axis=-1)
    summed = jnp.einsum(
        "hqk,khe->hqe", weight.astype(jnp.bfloat16), values, preferred_element_type=jnp.float32
    )
    attended = (summed / total[:, :, None]).astype(jnp.bfloat16)
    attended = jnp.transpose(attended, (1, 0, 2)).reshape(rows, group)
    mlp_term = lax.dot_general(
        mlp_act,
        lax.all_gather(w_mlp_back, "seq", axis=0, tiled=True),
        (((1,), (1,)), ((), ())),
        preferred_element_type=jnp.float32,
    )
    partial_term = jnp.dot(attended, w_out, preferred_element_type=jnp.float32) + mlp_term
    branch = lax.psum_scatter(
        partial_term.astype(jnp.bfloat16), "tp", scatter_dimension=1, tiled=True
    ).astype(jnp.float32)
    own_half = (hidden.astype(jnp.float32) + gate * branch).astype(jnp.bfloat16)
    split_width = local_width // 2
    guide_index = lax.axis_index("guide")
    kept = lax.dynamic_slice_in_dim(own_half, guide_index * split_width, split_width, 1)
    handed = lax.dynamic_slice_in_dim(own_half, (1 - guide_index) * split_width, split_width, 1)
    other_half = from_partner(handed, "guide", 0)
    is_cond = guide_index == 0
    cond = jnp.where(is_cond, kept, other_half).astype(jnp.float32)
    uncond = jnp.where(is_cond, other_half, kept).astype(jnp.float32)
    guided = (uncond + guidance * (cond - uncond)).astype(jnp.bfloat16)
    return guided.reshape(rows, 1, 1, split_width)


def solution(mesh):
    in_specs = (
        P("seq", "tp"),
        P("seq"),
        P("guide", None, None, None),
        P(),
        P(None, None, "tp"),
        P("seq", "tp"),
        P("tp", None),
        P("seq", "tp"),
    )
    out_specs = P("seq", "tp", "guide", None)
    return jax.shard_map(
        on_device, mesh=mesh, in_specs=in_specs, out_specs=out_specs, check_vma=False
    )
```

profile of v0, /device:TPU:6, one launch (start us, length us, event | category | flops | bytes accessed | tf_op | source)
XLA Modules:
  0.0 259.2 jit_solution(889151841724916340)
XLA Ops:
  6.5 0.0 copy-start
  6.5 0.0 all-gather.4.cloned.1.call-start
  6.5 19.1 %all_gather.16 = bf16[64,3072]{1,0:T(8,128)(2,1)S(1)} all-gather(bf16[64,768]{1,0:T(8,128)(2,1)} %param.8), channel_id=1, replica_groups=mesh['guide'=2,'seq'=32,'tp'=4] {'tp'}, dimensions={1}, use_global_device_ids=true | all-gather | bytes 491520 | tf_op jit(solution)/shard_map/all_gather | solution.py:32
  25.6 0.2 convert_reduce_fusion
  25.8 0.3 fusion.11
  26.1 0.8 slice.35
  26.9 1.1 fusion.42
  28.0 0.2 fusion.14
  28.2 0.0 copy-start.3
  28.2 4.3 %fusion.25 = f32[64,3,384]{2,0,1:T(8,128)S(1)} fusion(bf16[3072,3,384]{2,0,1:T(8,128)(2,1)} %param.12, bf16[64,3072]{1,0:T(8,128)(2,1)S(1)} %fusion.14), kind=kOutput, calls=%fused_computation.33 | convolution fusion | flops 452984832 | bytes 7766016 | tf_op jit(solution)/shard_map/td,dck->tck/dot_general | solution.py:50
  32.5 0.0 copy-start.4
  32.5 0.0 copy-start.2
  32.7 0.1 reduce_sum.48
  32.9 0.1 mul.133
  33.0 0.7 pad_maximum_fusion
  33.7 0.0 all-gather.4.cloned.1.call-update
  33.7 0.0 all-gather.6.cloned.1.call-start
  33.7 0.7 all-gather.6.cloned.1.call-update
  34.4 0.0 all-gather.8.cloned.1.call-start
  34.5 0.7 all-gather.8.cloned.1.call-update
  35.2 0.0 reduce-scatter.2.cloned.1.call-start
  35.3 0.0 copy-done.4
  35.3 0.6 dynamic-slice.1
  36.6 0.1 broadcast_add_fusion
  36.7 14.9 %all-reduce = s32[2048]{0:T(1024)S(1)} all-reduce(s32[2048]{0:T(1024)S(1)} %get-tuple-element.12), channel_id=1, replica_groups=mesh['guide'=2,'seq'=32,'tp'=4] {'seq'}, use_global_device_ids=true, to_apply=%add | all-reduce | flops 2048 | bytes 16384
  51.6 0.1 multiply_reduce_fusion
  51.8 0.1 multiply_convert_fusion
  51.9 0.1 broadcast_compare_fusion
  52.0 30.8 %all-gather.4.cloned.1.call-done = bf16[2048,768]{1,0:T(8,128)(2,1)} async-done(((bf16[64,768]{1,0:T(8,128)(2,1)}), bf16[2048,768]{1,0:T(8,128)(2,1)}) %all-gather.4.cloned.1.call-update) | async-done | bytes 3145744 | tf_op jit(solution)/shard_map/all_gather | solution.py:58
  82.8 3.9 %fusion.53 = (bf16[2048,384]{1,0:T(8,128)(2,1)}, bf16[2048,384]{1,0:T(8,128)(2,1)}) fusion(bf16[2048,768]{1,0:T(8,128)(2,1)} %all-gather.4.cloned.1.call-done), kind=kLoop, calls=%fused_computation.79 | loop fusion | bytes 6291456 | tf_op jit(solution)/shard_map/slice | solution.py:61
  86.7 2.6 %copy.31 = bf16[2048,384]{0,1:T(8,128)(2,1)} copy(bf16[2048,384]{1,0:T(8,128)(2,1)} %get-tuple-element.5) | data formatting | bytes 3145728 | tf_op jit(solution)/shard_map/slice | solution.py:61
  89.3 2.6 %copy.34 = bf16[2048,384]{0,1:T(8,128)(2,1)} copy(bf16[2048,384]{1,0:T(8,128)(2,1)} %get-tuple-element.6) | data formatting | bytes 3145728 | tf_op jit(solution)/shard_map/slice | solution.py:62
  92.0 2.0 fusion.55
  94.0 0.4 fusion.2
  94.3 1.0 copy-done.1
  95.4 0.7 fusion.8
  96.1 0.0 copy-done
  96.1 0.5 fusion.38
  96.7 49.0 %all-gather.6.cloned.1.call-done = bf16[3072,1536]{1,0:T(8,128)(2,1)} async-done(((bf16[96,1536]{1,0:T(8,128)(2,1)}), bf16[3072,1536]{1,0:T(8,128)(2,1)}) %all-gather.6.cloned.1.call-update) | async-done | bytes 9437200 | tf_op jit(solution)/shard_map/all_gather | solution.py:46
  145.7 62.7 %all-gather.8.cloned.1.call-done = bf16[3072,1536]{1,0:T(8,128)(2,1)} async-done(((bf16[96,1536]{1,0:T(8,128)(2,1)}), bf16[3072,1536]{1,0:T(8,128)(2,1)}) %all-gather.8.cloned.1.call-update) | async-done | bytes 9437200 | tf_op jit(solution)/shard_map/all_gather | solution.py:77
  208.3 11.7 %fusion = bf16[64,3072]{1,0:T(8,128)(2,1)} fusion(f32[64,3072]{1,0:T(8,128)S(1)} %fusion.38, bf16[3072,1536]{1,0:T(8,128)(2,1)} %all-gather.8.cloned.1.call-done, bf16[64,3072]{1,0:T(8,128)(2,1)S(1)} %fusion.14, bf16[3072,1536]{1,0:T(8,128)(2,1)} %all-gather.6.cloned.1.call-done), kind=kOutput, calls=%fused_computation.1 | convolution fusion | flops 1209237504 | bytes 20447232 | tf_op jit(solution)/shard_map/dot_general | solution.py:75
  220.0 0.0 reduce-scatter.2.cloned.1.call-update
  220.0 0.8 slice.34
  220.8 25.8 %reduce-scatter.2.cloned.1.call-done = bf16[64,768]{1,0:T(8,128)(2,1)} async-done(((bf16[64,3072]{1,0:T(8,128)(2,1)}), bf16[64,768]{1,0:T(8,128)(2,1)}) %reduce-scatter.2.cloned.1.call-update) | async-done | bytes 98320 | tf_op jit(solution)/shard_map/reduce_scatter | solution.py:82
  246.6 1.2 fusion.5
  247.8 0.6 collective-permute-start
  248.4 3.6 %collective-permute-done = bf16[64,384]{1,0:T(8,128)(2,1)S(1)} collective-permute-done((bf16[64,384]{1,0:T(8,128)(2,1)S(1)}, bf16[64,384]{1,0:T(8,128)(2,1)S(1)}, u32[]{:S(2)}, u32[]{:S(2)}) %collective-permute-start) | collective-permute-done | bytes 49184 | tf_op jit(solution)/shard_map/ppermute | solution.py:18
  252.0 0.6 fusion.37
  (16 shorter events, 0.2 us)
Async XLA Ops:
  6.5 89.6 %copy-start = (bf16[384,3072]{1,0:T(8,128)(2,1)S(1)}, bf16[384,3072]{1,0:T(8,128)(2,1)}, u32[]{:S(2)}) copy-start(bf16[384,3072]{1,0:T(8,128)(2,1)} %param.14) | copy-start | bytes 7077892
  6.5 76.3 %all-gather.4.cloned.1.call-start = ((), (), s32[]{:S(2)}) async-start(), calls=%async_computation.1 | async-start | bytes 3244032 | tf_op jit(solution)/shard_map/all_gather | solution.py:58
  28.2 4.6 %copy-start.3 = (f32[2,128]{1,0:T(2,128)S(1)}, f32[2,128]{1,0:T(2,128)}, u32[]{:S(2)}) copy-start(f32[2,128]{1,0:T(2,128)} %param.11) | copy-start | bytes 3076
  32.5 2.7 %copy-start.4 = (u32[256]{0:T(256)S(1)}, u32[256]{0:T(256)}, u32[]{:S(2)}) copy-start(u32[256]{0:T(256)} %constant.55) | copy-start | bytes 3076
  32.5 4.0 %copy-start.2 = (s32[64]{0:T(128)S(1)}, s32[64]{0:T(128)}, u32[]{:S(2)}) copy-start(s32[64]{0:T(128)} %param.9) | copy-start | bytes 772
  33.7 112.0 %all-gather.6.cloned.1.call-start = ((), (), s32[]{:S(2)}) async-start(), calls=%async_computation.2 | async-start | bytes 9732096 | tf_op jit(solution)/shard_map/all_gather | solution.py:46
  34.4 173.9 %all-gather.8.cloned.1.call-start = ((), (), s32[]{:S(2)}) async-start(), calls=%async_computation.3 | async-start | bytes 9732096 | tf_op jit(solution)/shard_map/all_gather | solution.py:77
  35.2 211.4 %reduce-scatter.2.cloned.1.call-start = ((), (), s32[]{:S(2)}) async-start(), calls=%async_computation.4 | async-start | bytes 491520 | tf_op jit(solution)/shard_map/reduce_scatter | solution.py:82
  94.0 1.4 copy-start.1
  247.8 4.2 %collective-permute-start = (bf16[64,384]{1,0:T(8,128)(2,1)S(1)}, bf16[64,384]{1,0:T(8,128)(2,1)S(1)}, u32[]{:S(2)}, u32[]{:S(2)}) collective-permute-start(bf16[64,384]{1,0:T(8,128)(2,1)S(1)} %constant_dynamic-slice_fusion), channel_id=1, source_target_pairs={{0,128},{128,0},{1,129},{129,1},{2,130},{130,2},{3,131},{131,3},{4... | collective-permute-start | bytes 147464 | tf_op jit(solution)/shard_map/ppermute | solution.py:18
Sparse Core Ops, SparseCore 0:
  33.8 48.9 all-gather.3
  85.3 60.2 all-gather.5
  148.2 60.0 all-gather.7
  220.2 26.4 reduce-scatter.1
where the time goes:
time: 260 us; the launch traced here: 259 us
  waiting for transfers between devices  173 us (67%)
  blocking collectives  34 us (13%)
  matrix products  21.4 us (8%)
  between operations  14 us (5%)
  local copies, waits for them, and re-layouts  12.6 us (5%)
  other arithmetic  3.08 us (1%)
    all_gather x1, waiting for transfers between devices, on_device(): lax.all_gather(w_mlp_back, 'seq', axis=0, tiled=True)  62.7 us
    all_gather x1, waiting for transfers between devices, on_device(): lax.all_gather(w_mlp_in, 'seq', axis=0, tiled=True)  49 us
    all_gather x1, waiting for transfers between devices, on_device(): keys_all = lax.all_gather(packed, 'seq', axis=0, tiled=True)  30.8 us
    reduce_scatter x1, waiting for transfers between devices, on_device(): lax.psum_scatter(partial_term.astype(jnp.bfloat16), 'tp', scatter_dimensi...  25.8 us
    all_gather x1, blocking collectives, on_device(): full = lax.all_gather(hidden, 'tp', axis=1, tiled=True)  19.1 us
    unnamed x1, blocking collectives  14.9 us
    dot_general x1, matrix products, on_device(): lax.dot_general(mlp_act, lax.all_gather(w_mlp_back, 'seq', axis=0, tiled=...  11.7 us
    slice x2, local copies, waits for them, and re-layouts, on_device(): keys = keys_all[:, :group].reshape(count, heads_here, HEAD)  6.53 us
  transfers between devices with their start and end apart: 5, of which 5 were waited for; matrix products, arithmetic and copies ran while one was open for 6% of the time, Pallas kernels for 0%

commit v1 on v0

--- a/solution.py
+++ b/solution.py
@@ -74,7 +74,9 @@
     attended = jnp.transpose(attended, (1, 0, 2)).reshape(rows, group)
     mlp_term = lax.dot_general(
         mlp_act,
-        lax.all_gather(w_mlp_back, "seq", axis=0, tiled=True),
+        jnp.concatenate(
+            lax.all_to_all(jnp.stack([w_mlp_back] * lax.axis_size("seq")), "seq", 0, 0), axis=0
+        ),
         (((1,), (1,)), ((), ())),
         preferred_element_type=jnp.float32,
     )

time: 260 us -> 286 us (1.10)
  blocking collectives: 34 us -> 147 us
  waiting for transfers between devices: 173 us -> 73 us
  starting transfers between devices: 0.68 us -> 8.44 us
  local copies, waits for them, and re-layouts: 12.6 us -> 18.3 us
    unnamed x1, blocking collectives: 14.9 us -> 128 us
    all_gather x1 -> x0, waiting for transfers between devices: 62.7 us -> none  [on_device(): lax.all_gather(w_mlp_back, 'seq', axis=0, tiled=True)]
    all_gather x1, waiting for transfers between devices: 30.8 us -> 0.02 us  [on_device(): keys_all = lax.all_gather(packed, 'seq', axis=0, tiled=True)]
    all_to_all x0 -> x1, starting transfers between devices: none -> 7.78 us  [on_device(): lax.all_to_all(jnp.stack([w_mlp_back] * lax.axis_size('seq')), 'seq', 0, 0)]
    all_gather x1, waiting for transfers between devices: 49 us -> 42.8 us  [on_device(): lax.all_gather(w_mlp_in, 'seq', axis=0, tiled=True)]
    another operation x0 -> x1, local copies, waits for them, and re-layouts: none -> 5.75 us  [on_device(): jnp.stack([w_mlp_back] * lax.axis_size('seq'))]
  transfers between devices with their start and end apart: 5 -> 5, of which waited for: 5 -> 3; matrix products, arithmetic and copies ran while one was open for 6% -> 7% of each run, Pallas kernels for 0% -> 0%
where the time goes in v1:
time: 286 us; the launch traced here: 285 us
  blocking collectives  147 us (51%)
  waiting for transfers between devices  73 us (26%)
  matrix products  21.5 us (8%)
  local copies, waits for them, and re-layouts  18.3 us (6%)
  between operations  14 us (5%)
  starting transfers between devices  8.44 us (3%)
  other arithmetic  3.06 us (1%)
    unnamed x1, blocking collectives  128 us
    all_gather x1, waiting for transfers between devices, on_device(): lax.all_gather(w_mlp_in, 'seq', axis=0, tiled=True)  42.8 us
    reduce_scatter x1, waiting for transfers between devices, on_device(): lax.psum_scatter(partial_term.astype(jnp.bfloat16), 'tp', scatter_dimensi...  25.8 us
    all_gather x1, blocking collectives, on_device(): full = lax.all_gather(hidden, 'tp', axis=1, tiled=True)  19.1 us
    dot_general x1, matrix products, on_device(): lax.dot_general(mlp_act, jnp.concatenate(lax.all_to_all(jnp.stack([w_mlp_...  11.7 us
    all_to_all x1, starting transfers between devices, on_device(): lax.all_to_all(jnp.stack([w_mlp_back] * lax.axis_size('seq')), 'seq', 0, 0)  7.78 us
    slice x2, local copies, waits for them, and re-layouts, on_device(): keys = keys_all[:, :group].reshape(count, heads_here, HEAD)  6.49 us
    another operation x1, local copies, waits for them, and re-layouts, on_device(): jnp.stack([w_mlp_back] * lax.axis_size('seq'))  5.75 us
  transfers between devices with their start and end apart: 5, of which 3 were waited for; matrix products, arithmetic and copies ran while one was open for 7% of the time, Pallas kernels for 0%

profile of v1, /device:TPU:6, one launch (start us, length us, event | category | flops | bytes accessed | tf_op | source)
XLA Modules:
  0.0 285.0 jit_solution(3949629765620992939)
XLA Ops:
  6.5 0.0 copy-start
  6.5 0.0 all-gather.3.cloned.1.call-start
  6.5 19.1 %all_gather.13 = bf16[64,3072]{1,0:T(8,128)(2,1)S(1)} all-gather(bf16[64,768]{1,0:T(8,128)(2,1)} %param.8), channel_id=1, replica_groups=mesh['guide'=2,'seq'=32,'tp'=4] {'tp'}, dimensions={1}, use_global_device_ids=true | all-gather | bytes 491520 | tf_op jit(solution)/shard_map/all_gather | solution.py:32
  25.6 0.2 convert_reduce_fusion
  25.8 0.3 fusion.11
  26.1 0.8 slice.35
  26.9 1.1 fusion.42
  28.0 0.2 fusion.14
  28.2 0.0 copy-start.3
  28.2 4.3 %fusion.25 = f32[64,3,384]{2,0,1:T(8,128)S(1)} fusion(bf16[3072,3,384]{2,0,1:T(8,128)(2,1)} %param.12, bf16[64,3072]{1,0:T(8,128)(2,1)S(1)} %fusion.14), kind=kOutput, calls=%fused_computation.33 | convolution fusion | flops 452984832 | bytes 7766016 | tf_op jit(solution)/shard_map/td,dck->tck/dot_general | solution.py:50
  32.6 0.1 reduce_sum.48
  32.8 0.0 copy-done.3
  32.8 0.1 mul.133
  33.0 0.6 pad_maximum_fusion
  33.6 0.0 all-gather.3.cloned.1.call-update
  33.6 0.0 all-gather.5.cloned.1.call-start
  33.7 0.7 all-gather.5.cloned.1.call-update
  34.4 5.8 %stack.2 = bf16[32,96,1536]{2,1,0:T(8,128)(2,1)} broadcast(bf16[96,1536]{1,0:T(8,128)(2,1)} %param.15), dimensions={1,2} | broadcast | bytes 9732096 | tf_op jit(solution)/shard_map/stack | solution.py:78
  40.1 7.8 %all-to-all-start = ((bf16[32,96,1536]{2,1,0:T(8,128)(2,1)}), bf16[32,96,1536]{2,1,0:T(8,128)(2,1)}, u32[]{:S(2)}, u32[]{:S(2)}) async-start(bf16[32,96,1536]{2,1,0:T(8,128)(2,1)} %stack.2), calls=%async_computation | async-start | bytes 18874368 | tf_op jit(solution)/shard_map/all_to_all | solution.py:78
  47.9 0.0 reduce-scatter.2.cloned.1.call-start
  48.1 0.0 copy-done.4
  48.1 0.6 dynamic-slice.1
  49.3 0.0 copy-done.2
  49.3 0.1 broadcast_add_fusion
  49.4 127.7 %all-reduce = s32[2048]{0:T(1024)S(1)} all-reduce(s32[2048]{0:T(1024)S(1)} %get-tuple-element.12), channel_id=1, replica_groups=mesh['guide'=2,'seq'=32,'tp'=4] {'seq'}, use_global_device_ids=true, to_apply=%add | all-reduce | flops 2048 | bytes 16384
  177.1 0.1 multiply_reduce_fusion
  177.3 0.1 multiply_convert_fusion
  177.4 0.1 broadcast_compare_fusion
  177.6 0.0 all-gather.3.cloned.1.call-done
  177.6 3.9 %fusion.53 = (bf16[2048,384]{1,0:T(8,128)(2,1)}, bf16[2048,384]{1,0:T(8,128)(2,1)}) fusion(bf16[2048,768]{1,0:T(8,128)(2,1)} %all-gather.3.cloned.1.call-done), kind=kLoop, calls=%fused_computation.79 | loop fusion | bytes 6291456 | tf_op jit(solution)/shard_map/slice | solution.py:61
  181.5 2.6 copy.31
  184.1 2.6 copy.34
  186.7 2.0 fusion.55
  188.7 0.0 copy-start.1
  188.7 0.4 fusion.2
  189.1 1.0 copy-done.1
  190.1 0.7 fusion.8
  190.9 0.5 fusion.38
  191.4 0.0 all-to-all-done
  191.4 42.8 %all-gather.5.cloned.1.call-done = bf16[3072,1536]{1,0:T(8,128)(2,1)} async-done(((bf16[96,1536]{1,0:T(8,128)(2,1)}), bf16[3072,1536]{1,0:T(8,128)(2,1)}) %all-gather.5.cloned.1.call-update) | async-done | bytes 9437200 | tf_op jit(solution)/shard_map/all_gather | solution.py:46
  234.2 11.7 %fusion = bf16[64,3072]{1,0:T(8,128)(2,1)} fusion(f32[64,3072]{1,0:T(8,128)S(1)} %fusion.38, bf16[3072,1536]{1,0:T(8,128)(2,1)} %bitcast.13, bf16[64,3072]{1,0:T(8,128)(2,1)S(1)} %fusion.14, bf16[3072,1536]{1,0:T(8,128)(2,1)} %all-gather.5.cloned.1.call-done), kind=kOutput, calls=%fused_computation.1 | convolution fusion | flops 1209237504 | bytes 20447232 | tf_op jit(solution)/shard_map/dot_general | solution.py:75
  245.9 0.0 reduce-scatter.2.cloned.1.call-update
  245.9 0.8 slice.34
  246.7 25.8 %reduce-scatter.2.cloned.1.call-done = bf16[64,768]{1,0:T(8,128)(2,1)} async-done(((bf16[64,3072]{1,0:T(8,128)(2,1)}), bf16[64,768]{1,0:T(8,128)(2,1)}) %reduce-scatter.2.cloned.1.call-update) | async-done | bytes 98320 | tf_op jit(solution)/shard_map/reduce_scatter | solution.py:84
  272.5 1.2 fusion.5
  273.7 0.6 collective-permute-start
  274.2 3.6 %collective-permute-done = bf16[64,384]{1,0:T(8,128)(2,1)S(1)} collective-permute-done((bf16[64,384]{1,0:T(8,128)(2,1)S(1)}, bf16[64,384]{1,0:T(8,128)(2,1)S(1)}, u32[]{:S(2)}, u32[]{:S(2)}) %collective-permute-start) | collective-permute-done | bytes 49184 | tf_op jit(solution)/shard_map/ppermute | solution.py:18
  277.9 0.6 fusion.37
  (16 shorter events, 0.2 us)
Async XLA Ops:
  6.5 184.3 %copy-start = (bf16[384,3072]{1,0:T(8,128)(2,1)S(1)}, bf16[384,3072]{1,0:T(8,128)(2,1)}, u32[]{:S(2)}) copy-start(bf16[384,3072]{1,0:T(8,128)(2,1)} %param.14) | copy-start | bytes 7077892
  6.5 171.1 %all-gather.3.cloned.1.call-start = ((), (), s32[]{:S(2)}) async-start(), calls=%async_computation.2 | async-start | bytes 3244032 | tf_op jit(solution)/shard_map/all_gather | solution.py:58
  28.2 4.6 %copy-start.3 = (f32[2,128]{1,0:T(2,128)S(1)}, f32[2,128]{1,0:T(2,128)}, u32[]{:S(2)}) copy-start(f32[2,128]{1,0:T(2,128)} %param.11) | copy-start | bytes 3076
  33.6 200.6 %all-gather.5.cloned.1.call-start = ((), (), s32[]{:S(2)}) async-start(), calls=%async_computation.3 | async-start | bytes 9732096 | tf_op jit(solution)/shard_map/all_gather | solution.py:46
  40.1 7.9 %copy-start.4 = (u32[256]{0:T(256)S(1)}, u32[256]{0:T(256)}, u32[]{:S(2)}) copy-start(u32[256]{0:T(256)} %constant.55) | copy-start | bytes 3076
  40.1 9.2 %copy-start.2 = (s32[64]{0:T(128)S(1)}, s32[64]{0:T(128)}, u32[]{:S(2)}) copy-start(s32[64]{0:T(128)} %param.9) | copy-start | bytes 772
  40.1 151.3 %all-to-all-start = ((bf16[32,96,1536]{2,1,0:T(8,128)(2,1)}), bf16[32,96,1536]{2,1,0:T(8,128)(2,1)}, u32[]{:S(2)}, u32[]{:S(2)}) async-start(bf16[32,96,1536]{2,1,0:T(8,128)(2,1)} %stack.2), calls=%async_computation | async-start | bytes 18874368 | tf_op jit(solution)/shard_map/all_to_all | solution.py:78
  47.9 224.5 %reduce-scatter.2.cloned.1.call-start = ((), (), s32[]{:S(2)}) async-start(), calls=%async_computation.4 | async-start | bytes 491520 | tf_op jit(solution)/shard_map/reduce_scatter | solution.py:84
  188.7 1.4 copy-start.1
  273.7 4.2 %collective-permute-start = (bf16[64,384]{1,0:T(8,128)(2,1)S(1)}, bf16[64,384]{1,0:T(8,128)(2,1)S(1)}, u32[]{:S(2)}, u32[]{:S(2)}) collective-permute-start(bf16[64,384]{1,0:T(8,128)(2,1)S(1)} %constant_dynamic-slice_fusion), channel_id=1, source_target_pairs={{0,128},{128,0},{1,129},{129,1},{2,130},{130,2},{3,131},{131,3},{4... | collective-permute-start | bytes 147464 | tf_op jit(solution)/shard_map/ppermute | solution.py:18
Sparse Core Ops, SparseCore 0:
  33.8 140.3 all-gather.2
  176.8 57.4 all-gather.4
  246.1 26.3 reduce-scatter.1
